TPU v7x, 256 devices: a whole 4x4x8 slice. The times are simulated.
256 devices in a mesh: ta: 4 (over z_lo, core), pa: 64 (over x, y, z_hi).
Axes of the slice: x: 4, y: 4, z: 8 (z_hi: 4, z_lo: 2; z = z_hi * 2 + z_lo), core: 2. Of those that a mesh axis runs over, the one named last changes fastest.
Arguments:
- green_freq: bfloat16 [256, 4, 256, 256], P('ta', None, 'pa'), may hold values from -6 to 6
- colloc: bfloat16 [4, 256, 1024], P(None, None, 'pa'), may hold values from -0.375 to 0.375
- core: bfloat16 [1024, 1024], replicated, may hold values from -0.1875 to 0.1875
Outputs:
- sigma_freq: bfloat16 [256, 4, 256, 256], P('ta', None, 'pa')
All inputs are finite; a program needn't handle non-finite values.
Results may differ from a plain program's by a relative error of at most 0.03.
Values may be sent and summed in bfloat16 or wider, within the bound.
No kernel may reach another device: no remote copies, remote signals or barrier semaphores. Data moves between devices by JAX's collectives and lax.ppermute only.
A program may use at most 128 MiB of HBM per device.

v0:
```python
import jax
import jax.numpy as jnp
from jax import lax
from jax.sharding import PartitionSpec as P

NFREQ = 128
NTIME = 128


def cut_along(array, dim, length):
    lengths = array.shape
    blocks = array.reshape(*lengths[:dim], length, lengths[dim] // length, *lengths[dim + 1 :])
    return jnp.moveaxis(blocks, dim, 0)


def summed_on_arrival(array, axis, dim):
    blocks = cut_along(array, dim, lax.axis_size(axis))
    arrived = lax.all_to_all(blocks, axis, split_axis=0, concat_axis=0, tiled=True)
    return arrived.astype(jnp.float32).sum(axis=0)


def time_tables(nfreq, ntime):
    freq = jnp.arange(nfreq, dtype=jnp.float32)
    times = jnp.arange(ntime, dtype=jnp.float32)
    phase = jnp.pi * (2.0 * freq[None, :] + 1.0) * (times[:, None] + 0.5) / ntime
    cosine = jnp.cos(phase)
    sine = jnp.sin(phase)
    scale_fwd = 1.0 / jnp.sqrt(jnp.float32(nfreq))
    scale_back = 1.0 / jnp.sqrt(jnp.float32(ntime))
    plus = jnp.concatenate([cosine, sine], axis=1) * scale_fwd
    minus = jnp.concatenate([-cosine, sine], axis=1) * scale_fwd
    fwd = jnp.stack([plus, minus], axis=0)
    back = jnp.concatenate([cosine.T, sine.T], axis=0) * scale_back
    return (fwd, back)


def local(green_freq, colloc, core):
    fwd, back = time_tables(NFREQ, NTIME)
    freq_rows = green_freq.shape[0]
    first = lax.axis_index("ta") * freq_rows
    fwd_part = lax.dynamic_slice_in_dim(fwd, first, freq_rows, 2)
    partial_time = jnp.einsum(
        "stw,wkij->stkij", fwd_part, green_freq.astype(jnp.float32), precision=lax.Precision.HIGHEST
    )
    green_time = summed_on_arrival(partial_time.astype(jnp.bfloat16), "ta", 1).astype(jnp.bfloat16)
    piece = lax.all_gather(colloc, "pa", axis=2, tiled=True)
    half_piece = jnp.einsum(
        "stkij,kjq->stkiq", green_time, piece, preferred_element_type=jnp.float32
    ).astype(jnp.bfloat16)
    gathered = piece[None, None]
    full_colloc = gathered[0, 0]
    kcount = full_colloc.shape[0]
    green_pts = jnp.einsum(
        "kip,stkiq->stkpq",
        full_colloc,
        lax.all_to_all(half_piece, "pa", split_axis=4, concat_axis=3, tiled=True),
        preferred_element_type=jnp.float32,
    )
    bubble_block = (jnp.sum(green_pts[0] * green_pts[1], axis=1) / kcount).astype(jnp.bfloat16)
    green_plus = green_pts[0]
    mixed = jnp.einsum(
        "pr,trq->tpq", core, bubble_block, preferred_element_type=jnp.float32
    ).astype(jnp.bfloat16)
    mixed_rows = lax.all_to_all(mixed, "pa", split_axis=1, concat_axis=2, tiled=True)
    screened_rows = jnp.einsum(
        "tps,sq->tpq", mixed_rows, core, preferred_element_type=jnp.float32
    ).astype(jnp.bfloat16)
    screened = lax.all_to_all(screened_rows, "pa", split_axis=2, concat_axis=1, tiled=True)
    source = (-green_plus * screened.astype(jnp.float32)[:, None]).astype(jnp.bfloat16)
    outer = jnp.einsum(
        "kip,tkpq->tkiq", full_colloc, source, preferred_element_type=jnp.float32
    ).astype(jnp.bfloat16)
    sigma_time = jnp.einsum(
        "tkiq,kjq->tkij",
        lax.all_to_all(outer, "pa", split_axis=2, concat_axis=3, tiled=True),
        full_colloc,
        preferred_element_type=jnp.float32,
    ).astype(jnp.bfloat16)
    time_rows = sigma_time.shape[0]
    first_time = lax.axis_index("ta") * time_rows
    back_part = lax.dynamic_slice_in_dim(back, first_time, time_rows, 1)
    partial_freq = jnp.einsum(
        "wt,tkij->wkij", back_part, sigma_time.astype(jnp.float32), precision=lax.Precision.HIGHEST
    )
    return summed_on_arrival(partial_freq.astype(jnp.bfloat16), "ta", 0).astype(jnp.bfloat16)


def solution(mesh):
    return jax.shard_map(
        local,
        mesh=mesh,
        in_specs=(P("ta", None, "pa", None), P(None, None, "pa"), P()),
        out_specs=P("ta", None, "pa", None),
        check_vma=False,
    )
```

profile of v0, /device:TPU:1, one launch (start us, length us, event | category | flops | bytes accessed | tf_op | source)
XLA Modules:
  0.0 482.5 jit_solution(289619318880138585)
XLA Ops:
  11.0 31.8 %all_to_all.73 = bf16[4,2,32,4,4,256]{5,2,4,3,1,0:T(8,128)(2,1)} all-to-all(bf16[4,2,32,4,4,256]{5,2,4,3,1,0:T(8,128)(2,1)S(1)} %bitcast.122), channel_id=1, replica_groups=mesh['ta'=4,'pa'=64] {'ta'}, dimensions={0} | all-to-all | bytes 4194304 | tf_op jit(solution)/shard_map/all_to_all | solution.py:18
  44.8 48.7 %all-gather.2.cloned.1.call-done = bf16[4,256,1024]{1,2,0:T(8,128)(2,1)} async-done(((bf16[4,256,16]{1,2,0:T(8,128)(2,1)}), bf16[4,256,1024]{1,2,0:T(8,128)(2,1)}) %all-gather.2.cloned.1.call-update) | async-done | bytes 2097168 | tf_op jit(solution)/shard_map/all_gather | solution.py:46
  93.5 3.7 convert_bitcast_fusion
  97.1 13.3 %copy.69 = bf16[2,32,4,4,1024]{1,3,0,2,4:T(4,128)(2,1)} copy(bf16[2,32,4,4,1024]{4,1,3,0,2:T(8,128)(2,1)} %convert_bitcast_fusion) | data formatting | bytes 4194304 | tf_op jit(solution)/shard_map/convert_element_type | solution.py:49
  110.4 13.7 %reshape.210 = bf16[64,2,8192]{2,1,0:T(2,128)(2,1)} reshape(bf16[1024,4,2,4,32]{4,3,2,1,0:T(4,128)(2,1)} %bitcast.106) | data formatting | bytes 4194304
  124.1 63.4 %all_to_all.74 = bf16[64,2,8192]{2,1,0:T(2,128)(2,1)} all-to-all(bf16[64,2,8192]{2,1,0:T(2,128)(2,1)} %reshape.210), channel_id=1, replica_groups=mesh['ta'=4,'pa'=64] {'pa'}, dimensions={0} | all-to-all | bytes 4194304 | tf_op jit(solution)/shard_map/all_to_all | solution.py:56
  187.5 13.3 %reshape.211 = bf16[1024,4,2,4,32]{4,3,2,1,0:T(4,128)(2,1)} reshape(bf16[64,2,8192]{2,1,0:T(2,128)(2,1)} %all_to_all.74) | data formatting | bytes 4194304
  200.8 9.8 %copy.70 = bf16[2,32,4,4,1024]{1,4,3,2,0:T(8,128)(2,1)} copy(bf16[2,32,4,4,1024]{1,3,0,2,4:T(4,128)(2,1)} %bitcast.107) | data formatting | bytes 4194304 | tf_op jit(solution)/shard_map/all_to_all | solution.py:56
  210.6 9.1 %copy.71 = bf16[2,32,4,64,4,16]{1,5,4,3,2,0:T(8,128)(2,1)} copy(bf16[2,32,4,64,4,16]{1,5,3,4,2,0:T(8,128)(2,1)} %bitcast.110) | data formatting | bytes 4194304 | tf_op jit(solution)/shard_map/all_to_all | solution.py:56
  219.7 11.9 %copy.72 = bf16[2,32,4,256,16]{3,4,1,0,2:T(8,128)(2,1)} copy(bf16[2,32,4,256,16]{1,4,3,2,0:T(8,128)(2,1)} %bitcast.108) | data formatting | bytes 4194304 | tf_op jit(solution)/shard_map/all_to_all | solution.py:56
  231.6 4.6 convolution_bitcast_fusion
  243.4 5.1 %copy.73 = bf16[32,1024,16]{0,2,1:T(8,128)(2,1)} copy(bf16[32,1024,16]{1,2,0:T(8,128)(2,1)S(1)} %fusion.28) | data formatting | bytes 2097152 | tf_op jit(solution)/shard_map/convert_element_type | solution.py:63
  248.5 6.4 %reshape.212 = bf16[64,2,4096]{2,1,0:T(2,128)(2,1)S(1)} reshape(bf16[1024,16,32]{2,1,0:T(8,128)(2,1)} %bitcast.113) | data formatting | bytes 2097152
  255.0 33.4 %all_to_all.75 = bf16[64,2,4096]{2,1,0:T(2,128)(2,1)} all-to-all(bf16[64,2,4096]{2,1,0:T(2,128)(2,1)S(1)} %reshape.212), channel_id=1, replica_groups=mesh['ta'=4,'pa'=64] {'pa'}, dimensions={0} | all-to-all | bytes 2097152 | tf_op jit(solution)/shard_map/all_to_all | solution.py:64
  288.4 6.5 %reshape.213 = bf16[1024,16,32]{2,1,0:T(8,128)(2,1)} reshape(bf16[64,2,4096]{2,1,0:T(2,128)(2,1)} %all_to_all.75) | data formatting | bytes 2097152
  294.9 5.2 %copy.74 = bf16[32,16,64,16]{0,3,2,1:T(8,128)(2,1)} copy(bf16[32,16,64,16]{0,3,1,2:T(8,128)(2,1)} %bitcast.117) | data formatting | bytes 2097152 | tf_op jit(solution)/shard_map/all_to_all | solution.py:64
  300.1 4.0 copy.75
  306.3 7.4 %copy.76 = bf16[32,16,1024]{0,1,2:T(8,128)(2,1)} copy(bf16[32,16,1024]{2,1,0:T(8,128)(2,1)} %fusion.25) | data formatting | bytes 2097152 | tf_op jit(solution)/shard_map/convert_element_type | solution.py:67
  313.7 6.4 %reshape.214 = bf16[64,2,4096]{2,1,0:T(2,128)(2,1)S(1)} reshape(bf16[1024,16,32]{2,1,0:T(8,128)(2,1)} %bitcast.114) | data formatting | bytes 2097152
  320.1 29.6 %all_to_all.76 = bf16[64,2,4096]{2,1,0:T(2,128)(2,1)S(1)} all-to-all(bf16[64,2,4096]{2,1,0:T(2,128)(2,1)S(1)} %reshape.214), channel_id=1, replica_groups=mesh['ta'=4,'pa'=64] {'pa'}, dimensions={0} | all-to-all | bytes 2097152 | tf_op jit(solution)/shard_map/all_to_all | solution.py:68
  349.7 3.5 reshape.215
  353.3 5.2 %copy.77 = bf16[32,16,1024]{2,1,0:T(8,128)(2,1)S(1)} copy(bf16[32,16,1024]{0,1,2:T(8,128)(2,1)} %bitcast.115) | data formatting | bytes 2097152 | tf_op jit(solution)/shard_map/all_to_all | solution.py:68
  358.5 4.2 copy.78
  362.7 7.8 %copy.79 = f32[32,64,16,16]{0,3,2,1:T(8,128)} copy(f32[32,64,16,16]{0,3,1,2:T(8,128)} %bitcast.111) | data formatting | bytes 4194304 | tf_op jit(solution)/shard_map/convert_element_type | solution.py:69
  370.6 6.8 %copy.80 = f32[32,1024,16]{1,2,0:T(8,128)} copy(f32[32,1024,16]{0,2,1:T(8,128)} %bitcast.109) | data formatting | bytes 4194304 | tf_op jit(solution)/shard_map/convert_element_type | solution.py:69
  377.4 5.2 %fusion.31 = bf16[32,4,256,16]{2,3,0,1:T(8,128)(2,1)S(1)} fusion(bf16[4,256,1024]{1,2,0:T(8,128)(2,1)S(1)} %copy-done.3, f32[2,32,4,1024,16]{3,4,1,0,2:T(8,128)} %copy-done.2, f32[32,1024,16]{1,2,0:T(8,128)} %copy.80), kind=kOutput, calls=%fused_computation.26 | convolution fusion | flops 1080557568 | bytes 13631488 | tf_op jit(solution)/shard_map/kip,tkpq->tkiq/dot_general | solution.py:70
  382.6 7.5 %copy.81 = bf16[32,4,256,16]{0,3,1,2:T(8,128)(2,1)} copy(bf16[32,4,256,16]{2,3,0,1:T(8,128)(2,1)S(1)} %fusion.31) | data formatting | bytes 2097152 | tf_op jit(solution)/shard_map/convert_element_type | solution.py:72
  390.1 7.3 %reshape.216 = bf16[64,2,4096]{2,1,0:T(2,128)(2,1)} reshape(bf16[256,4,16,32]{3,2,1,0:T(8,128)(2,1)} %bitcast.116) | data formatting | bytes 2097152
  397.3 6.5 %all-to-all-start.4 = ((bf16[64,2,4096]{2,1,0:T(2,128)(2,1)}), bf16[64,2,4096]{2,1,0:T(2,128)(2,1)S(1)}, u32[]{:S(2)}, u32[]{:S(2)}) async-start(bf16[64,2,4096]{2,1,0:T(2,128)(2,1)} %reshape.216), calls=%async_computation.4 | async-start | bytes 2097152 | tf_op jit(solution)/shard_map/all_to_all | solution.py:75
  403.8 21.3 %all-to-all-done.4 = bf16[64,2,4096]{2,1,0:T(2,128)(2,1)S(1)} async-done(((bf16[64,2,4096]{2,1,0:T(2,128)(2,1)}), bf16[64,2,4096]{2,1,0:T(2,128)(2,1)S(1)}, u32[]{:S(2)}, u32[]{:S(2)}) %all-to-all-start.4) | async-done | bytes 1048608 | tf_op jit(solution)/shard_map/all_to_all | solution.py:75
  425.1 3.5 reshape.217
  435.2 36.9 %all_to_all.77 = bf16[4,64,4,4,256]{4,1,3,2,0:T(8,128)(2,1)} all-to-all(bf16[4,64,4,4,256]{4,1,3,2,0:T(8,128)(2,1)S(1)} %copy.85), channel_id=1, replica_groups=mesh['ta'=4,'pa'=64] {'ta'}, dimensions={0} | all-to-all | bytes 4194304 | tf_op jit(solution)/shard_map/all_to_all | solution.py:18
  (25 shorter events, 25.6 us)
Async XLA Ops:
  6.5 235.6 %copy-start = (bf16[1024,1024]{1,0:T(8,128)(2,1)S(1)}, bf16[1024,1024]{1,0:T(8,128)(2,1)}, u32[]{:S(2)}) copy-start(bf16[1024,1024]{1,0:T(8,128)(2,1)} %param.5) | copy-start | bytes 6291460
  6.5 86.9 %all-gather.2.cloned.1.call-start = ((), (), s32[]{:S(2)}) async-start(), calls=%async_computation.6 | async-start | bytes 2129920 | tf_op jit(solution)/shard_map/all_gather | solution.py:46
  236.2 5.8 %copy-start.2 = (f32[2,32,4,1024,16]{3,4,1,0,2:T(8,128)}, f32[2,32,4,1024,16]{3,4,1,0,2:T(8,128)S(1)}, u32[]{:S(2)}) copy-start(f32[2,32,4,1024,16]{3,4,1,0,2:T(8,128)S(1)} %convolution_bitcast_fusion) | copy-start | bytes 50331652
  370.6 6.8 %copy-start.3 = (bf16[4,256,1024]{1,2,0:T(8,128)(2,1)S(1)}, bf16[4,256,1024]{1,2,0:T(8,128)(2,1)}, u32[]{:S(2)}) copy-start(bf16[4,256,1024]{1,2,0:T(8,128)(2,1)} %all-gather.2.cloned.1.call-done) | copy-start | bytes 6291460
  397.3 27.8 %all-to-all-start.4 = ((bf16[64,2,4096]{2,1,0:T(2,128)(2,1)}), bf16[64,2,4096]{2,1,0:T(2,128)(2,1)S(1)}, u32[]{:S(2)}, u32[]{:S(2)}) async-start(bf16[64,2,4096]{2,1,0:T(2,128)(2,1)} %reshape.216), calls=%async_computation.4 | async-start | bytes 2097152 | tf_op jit(solution)/shard_map/all_to_all | solution.py:75
  435.2 40.1 %copy-start.1 = (bf16[1024,1024]{1,0:T(8,128)(2,1)S(1)}, bf16[1024,1024]{1,0:T(8,128)(2,1)}, u32[]{:S(2)}) copy-start(bf16[1024,1024]{1,0:T(8,128)(2,1)} %param.5) | copy-start | bytes 6291460
Sparse Core Ops, SparseCore 0:
  10.5 82.9 all-gather.1
where the time goes:
time: 490 us; the launch traced here: 482 us
  blocking collectives  195 us (40%)
  local copies, waits for them, and re-layouts  166 us (34%)
  waiting for transfers between devices  70.7 us (14%)
  matrix products  23.1 us (5%)
  between operations  13.8 us (3%)
  other arithmetic  7.12 us (1%)
  starting transfers between devices  6.46 us (1%)
    all_to_all x2, blocking collectives, summed_on_arrival(): lax.all_to_all(blocks, axis, split_axis=0, concat_axis=0, tiled=True)  68.6 us
    unnamed x16, local copies, waits for them, and re-layouts  64 us
    all_to_all x1, blocking collectives, local(): lax.all_to_all(half_piece, 'pa', split_axis=4, concat_axis=3, tiled=True)  63.4 us
    all_gather x1, waiting for transfers between devices, local(): piece = lax.all_gather(colloc, 'pa', axis=2, tiled=True)  48.7 us
    all_to_all x1, blocking collectives, local(): lax.all_to_all(mixed, 'pa', split_axis=1, concat_axis=2, tiled=True)  33.4 us
    all_to_all x3, local copies, waits for them, and re-layouts, local(): lax.all_to_all(half_piece, 'pa', split_axis=4, concat_axis=3, tiled=True)  30.9 us
    all_to_all x1, blocking collectives, local(): lax.all_to_all(screened_rows, 'pa', split_axis=2, concat_axis=1, tiled=True)  29.6 us
    all_to_all x1, waiting for transfers between devices, local(): lax.all_to_all(outer, 'pa', split_axis=2, concat_axis=3, tiled=True)  21.3 us
  transfers between devices with their start and end apart: 2, of which 2 were waited for; matrix products, arithmetic and copies ran while one was open for 1% of the time, Pallas kernels for 0%

commit v1 on v0

--- a/solution.py
+++ b/solution.py
@@ -5,6 +5,12 @@
 
 NFREQ = 128
 NTIME = 128
+
+
+def load_sheet_now(block_here, d0):
+    return jnp.concatenate(
+        lax.all_to_all(jnp.stack(lax.axis_size("pa") * [block_here], axis=0), "pa", 0, 0), axis=d0
+    )
 
 
 def cut_along(array, dim, length):
@@ -43,7 +49,7 @@
         "stw,wkij->stkij", fwd_part, green_freq.astype(jnp.float32), precision=lax.Precision.HIGHEST
     )
     green_time = summed_on_arrival(partial_time.astype(jnp.bfloat16), "ta", 1).astype(jnp.bfloat16)
-    piece = lax.all_gather(colloc, "pa", axis=2, tiled=True)
+    piece = load_sheet_now(colloc, 2)
     half_piece = jnp.einsum(
         "stkij,kjq->stkiq", green_time, piece, preferred_element_type=jnp.float32
     ).astype(jnp.bfloat16)

time: 490 us -> 481 us (0.982)
  blocking collectives: 195 us -> 180 us
  between operations: 13.8 us -> 0.65 us
  starting transfers between devices: 6.46 us -> 19.4 us
  local copies, waits for them, and re-layouts: 166 us -> 174 us
    all_to_all x0 -> x1, waiting for transfers between devices: none -> 50.2 us  [load_sheet_now(): lax.all_to_all(jnp.stack(lax.axis_size('pa') * [block_here], axis=0), 'pa...]
    all_gather x1 -> x0, waiting for transfers between devices: 48.7 us -> none  [local(): piece = lax.all_gather(colloc, 'pa', axis=2, tiled=True)]
    all_to_all x0 -> x1, starting transfers between devices: none -> 12.8 us  [load_sheet_now(): lax.all_to_all(jnp.stack(lax.axis_size('pa') * [block_here], axis=0), 'pa...]
    all_to_all x1, blocking collectives: 63.4 us -> 52.8 us  [local(): lax.all_to_all(half_piece, 'pa', split_axis=4, concat_axis=3, tiled=True)]
    unnamed x16 -> x18, local copies, waits for them, and re-layouts: 64 us -> 68.3 us
  transfers between devices with their start and end apart: 2 -> 2, of which waited for: 2 -> 2; matrix products, arithmetic and copies ran while one was open for 1% -> 0% of each run, Pallas kernels for 0% -> 0%
where the time goes in v1:
time: 481 us; the launch traced here: 472 us
  blocking collectives  180 us (37%)
  local copies, waits for them, and re-layouts  174 us (36%)
  waiting for transfers between devices  69.1 us (14%)
  matrix products  22.1 us (5%)
  starting transfers between devices  19.4 us (4%)
  other arithmetic  7.12 us (1%)
    all_to_all x2, blocking collectives, summed_on_arrival(): lax.all_to_all(blocks, axis, split_axis=0, concat_axis=0, tiled=True)  68.9 us
    unnamed x18, local copies, waits for them, and re-layouts  68.3 us
    all_to_all x1, blocking collectives, local(): lax.all_to_all(half_piece, 'pa', split_axis=4, concat_axis=3, tiled=True)  52.8 us
    all_to_all x1, waiting for transfers between devices, load_sheet_now(): lax.all_to_all(jnp.stack(lax.axis_size('pa') * [block_here], axis=0), 'pa...  50.2 us
    all_to_all x1, blocking collectives, local(): lax.all_to_all(mixed, 'pa', split_axis=1, concat_axis=2, tiled=True)  30.9 us
    all_to_all x3, local copies, waits for them, and re-layouts, local(): lax.all_to_all(half_piece, 'pa', split_axis=4, concat_axis=3, tiled=True)  30.9 us
    all_to_all x1, blocking collectives, local(): lax.all_to_all(screened_rows, 'pa', split_axis=2, concat_axis=1, tiled=True)  27.5 us
    all_to_all x1, waiting for transfers between devices, local(): lax.all_to_all(outer, 'pa', split_axis=2, concat_axis=3, tiled=True)  19 us
  transfers between devices with their start and end apart: 2, of which 2 were waited for; matrix products, arithmetic and copies ran while one was open for 0% of the time, Pallas kernels for 0%

profile of v1, /device:TPU:1, one launch (start us, length us, event | category | flops | bytes accessed | tf_op | source)
XLA Modules:
  0.0 472.5 jit_solution(12471868017579000487)
XLA Ops:
  3.8 31.1 %all_to_all.78 = bf16[4,2,32,4,4,256]{5,2,4,3,1,0:T(8,128)(2,1)} all-to-all(bf16[4,2,32,4,4,256]{5,2,4,3,1,0:T(8,128)(2,1)S(1)} %bitcast.119), channel_id=1, replica_groups=mesh['ta'=4,'pa'=64] {'ta'}, dimensions={0} | all-to-all | bytes 4194304 | tf_op jit(solution)/shard_map/all_to_all | solution.py:24
  36.4 12.8 %all-to-all-start.1 = ((bf16[64,4,256,16]{2,3,1,0:T(8,128)(2,1)}), bf16[64,4,256,16]{2,3,1,0:T(8,128)(2,1)}, u32[]{:S(2)}, u32[]{:S(2)}) async-start(bf16[64,4,256,16]{2,3,1,0:T(8,128)(2,1)} %stack.5), calls=%async_computation.1 | async-start | bytes 4194304 | tf_op jit(solution)/shard_map/all_to_all | solution.py:12
  51.3 50.2 %all-to-all-done.1 = bf16[64,4,256,16]{2,3,1,0:T(8,128)(2,1)} async-done(((bf16[64,4,256,16]{2,3,1,0:T(8,128)(2,1)}), bf16[64,4,256,16]{2,3,1,0:T(8,128)(2,1)}, u32[]{:S(2)}, u32[]{:S(2)}) %all-to-all-start.1) | async-done | bytes 2097184 | tf_op jit(solution)/shard_map/all_to_all | solution.py:12
  106.6 13.3 %copy.85 = bf16[2,32,4,4,1024]{1,3,0,2,4:T(4,128)(2,1)} copy(bf16[2,32,4,4,1024]{4,1,3,0,2:T(8,128)(2,1)} %convert_bitcast_fusion) | data formatting | bytes 4194304 | tf_op jit(solution)/shard_map/convert_element_type | solution.py:55
  119.9 13.7 %reshape.219 = bf16[64,2,8192]{2,1,0:T(2,128)(2,1)} reshape(bf16[1024,4,2,4,32]{4,3,2,1,0:T(4,128)(2,1)} %bitcast.103) | data formatting | bytes 4194304
  133.6 52.8 %all_to_all.79 = bf16[64,2,8192]{2,1,0:T(2,128)(2,1)} all-to-all(bf16[64,2,8192]{2,1,0:T(2,128)(2,1)} %reshape.219), channel_id=1, replica_groups=mesh['ta'=4,'pa'=64] {'pa'}, dimensions={0} | all-to-all | bytes 4194304 | tf_op jit(solution)/shard_map/all_to_all | solution.py:62
  186.4 13.3 %reshape.220 = bf16[1024,4,2,4,32]{4,3,2,1,0:T(4,128)(2,1)} reshape(bf16[64,2,8192]{2,1,0:T(2,128)(2,1)} %all_to_all.79) | data formatting | bytes 4194304
  199.7 9.8 %copy.86 = bf16[2,32,4,4,1024]{1,4,3,2,0:T(8,128)(2,1)} copy(bf16[2,32,4,4,1024]{1,3,0,2,4:T(4,128)(2,1)} %bitcast.104) | data formatting | bytes 4194304 | tf_op jit(solution)/shard_map/all_to_all | solution.py:62
  209.5 9.1 %copy.87 = bf16[2,32,4,64,4,16]{1,5,4,3,2,0:T(8,128)(2,1)} copy(bf16[2,32,4,64,4,16]{1,5,3,4,2,0:T(8,128)(2,1)} %bitcast.107) | data formatting | bytes 4194304 | tf_op jit(solution)/shard_map/all_to_all | solution.py:62
  218.6 11.9 %copy.88 = bf16[2,32,4,256,16]{3,4,1,0,2:T(8,128)(2,1)} copy(bf16[2,32,4,256,16]{1,4,3,2,0:T(8,128)(2,1)} %bitcast.105) | data formatting | bytes 4194304 | tf_op jit(solution)/shard_map/all_to_all | solution.py:62
  230.5 4.6 convolution_bitcast_fusion
  242.3 5.1 %copy.90 = bf16[32,1024,16]{0,2,1:T(8,128)(2,1)} copy(bf16[32,1024,16]{1,2,0:T(8,128)(2,1)S(1)} %fusion.18) | data formatting | bytes 2097152 | tf_op jit(solution)/shard_map/convert_element_type | solution.py:69
  247.4 6.4 %reshape.221 = bf16[64,2,4096]{2,1,0:T(2,128)(2,1)S(1)} reshape(bf16[1024,16,32]{2,1,0:T(8,128)(2,1)} %bitcast.110) | data formatting | bytes 2097152
  253.9 30.9 %all_to_all.80 = bf16[64,2,4096]{2,1,0:T(2,128)(2,1)} all-to-all(bf16[64,2,4096]{2,1,0:T(2,128)(2,1)S(1)} %reshape.221), channel_id=1, replica_groups=mesh['ta'=4,'pa'=64] {'pa'}, dimensions={0} | all-to-all | bytes 2097152 | tf_op jit(solution)/shard_map/all_to_all | solution.py:70
  284.8 6.5 %reshape.222 = bf16[1024,16,32]{2,1,0:T(8,128)(2,1)} reshape(bf16[64,2,4096]{2,1,0:T(2,128)(2,1)} %all_to_all.80) | data formatting | bytes 2097152
  291.3 5.2 %copy.91 = bf16[32,16,64,16]{0,3,2,1:T(8,128)(2,1)} copy(bf16[32,16,64,16]{0,3,1,2:T(8,128)(2,1)} %bitcast.114) | data formatting | bytes 2097152 | tf_op jit(solution)/shard_map/all_to_all | solution.py:70
  296.6 4.0 copy.92
  302.7 7.4 %copy.93 = bf16[32,16,1024]{0,1,2:T(8,128)(2,1)} copy(bf16[32,16,1024]{2,1,0:T(8,128)(2,1)} %fusion.15) | data formatting | bytes 2097152 | tf_op jit(solution)/shard_map/convert_element_type | solution.py:73
  310.1 6.4 %reshape.223 = bf16[64,2,4096]{2,1,0:T(2,128)(2,1)S(1)} reshape(bf16[1024,16,32]{2,1,0:T(8,128)(2,1)} %bitcast.111) | data formatting | bytes 2097152
  316.6 27.5 %all_to_all.81 = bf16[64,2,4096]{2,1,0:T(2,128)(2,1)} all-to-all(bf16[64,2,4096]{2,1,0:T(2,128)(2,1)S(1)} %reshape.223), channel_id=1, replica_groups=mesh['ta'=4,'pa'=64] {'pa'}, dimensions={0} | all-to-all | bytes 2097152 | tf_op jit(solution)/shard_map/all_to_all | solution.py:74
  344.0 6.5 %reshape.224 = bf16[1024,16,32]{2,1,0:T(8,128)(2,1)} reshape(bf16[64,2,4096]{2,1,0:T(2,128)(2,1)} %all_to_all.81) | data formatting | bytes 2097152
  350.6 5.2 %copy.94 = bf16[32,16,1024]{2,1,0:T(8,128)(2,1)S(1)} copy(bf16[32,16,1024]{0,1,2:T(8,128)(2,1)} %bitcast.112) | data formatting | bytes 2097152 | tf_op jit(solution)/shard_map/all_to_all | solution.py:74
  355.8 4.2 copy.95
  360.1 7.8 %copy.96 = f32[32,64,16,16]{0,3,2,1:T(8,128)} copy(f32[32,64,16,16]{0,3,1,2:T(8,128)} %bitcast.108) | data formatting | bytes 4194304 | tf_op jit(solution)/shard_map/convert_element_type | solution.py:75
  367.9 6.6 %copy.97 = f32[32,1024,16]{1,2,0:T(8,128)} copy(f32[32,1024,16]{0,2,1:T(8,128)} %bitcast.106) | data formatting | bytes 4194304 | tf_op jit(solution)/shard_map/convert_element_type | solution.py:75
  374.5 5.8 %fusion.21 = bf16[32,4,256,16]{2,3,0,1:T(8,128)(2,1)S(1)} fusion(bf16[4,256,1024,1]{1,2,3,0:T(8,128)(2,1)} %bitcast.101, f32[2,32,4,1024,16]{3,4,1,0,2:T(8,128)} %copy-done.1, f32[32,1024,16]{1,2,0:T(8,128)} %copy.97), kind=kOutput, calls=%fused_computation.20 | convolution fusion | flops 1080557568 | bytes 13631488 | tf_op jit(solution)/shard_map/kip,tkpq->tkiq/dot_general | solution.py:76
  380.3 7.5 %copy.99 = bf16[32,4,256,16]{0,3,1,2:T(8,128)(2,1)} copy(bf16[32,4,256,16]{2,3,0,1:T(8,128)(2,1)S(1)} %fusion.21) | data formatting | bytes 2097152 | tf_op jit(solution)/shard_map/convert_element_type | solution.py:78
  387.8 7.3 %reshape.225 = bf16[64,2,4096]{2,1,0:T(2,128)(2,1)} reshape(bf16[256,4,16,32]{3,2,1,0:T(8,128)(2,1)} %bitcast.113) | data formatting | bytes 2097152
  395.1 6.6 %all-to-all-start.5 = ((bf16[64,2,4096]{2,1,0:T(2,128)(2,1)}), bf16[64,2,4096]{2,1,0:T(2,128)(2,1)S(1)}, u32[]{:S(2)}, u32[]{:S(2)}) async-start(bf16[64,2,4096]{2,1,0:T(2,128)(2,1)} %reshape.225), calls=%async_computation.5 | async-start | bytes 2097152 | tf_op jit(solution)/shard_map/all_to_all | solution.py:81
  401.6 19.0 %all-to-all-done.5 = bf16[64,2,4096]{2,1,0:T(2,128)(2,1)S(1)} async-done(((bf16[64,2,4096]{2,1,0:T(2,128)(2,1)}), bf16[64,2,4096]{2,1,0:T(2,128)(2,1)S(1)}, u32[]{:S(2)}, u32[]{:S(2)}) %all-to-all-start.5) | async-done | bytes 1048608 | tf_op jit(solution)/shard_map/all_to_all | solution.py:81
  420.6 3.5 reshape.226
  431.0 37.9 %all_to_all.82 = bf16[4,64,4,4,256]{4,1,3,2,0:T(8,128)(2,1)} all-to-all(bf16[4,64,4,4,256]{4,1,3,2,0:T(8,128)(2,1)S(1)} %copy.104), channel_id=1, replica_groups=mesh['ta'=4,'pa'=64] {'ta'}, dimensions={0} | all-to-all | bytes 4194304 | tf_op jit(solution)/shard_map/all_to_all | solution.py:24
  (28 shorter events, 31.9 us)
Async XLA Ops:
  0.0 241.0 %copy-start = (bf16[1024,1024]{1,0:T(8,128)(2,1)S(1)}, bf16[1024,1024]{1,0:T(8,128)(2,1)}, u32[]{:S(2)}) copy-start(bf16[1024,1024]{1,0:T(8,128)(2,1)} %param.5) | copy-start | bytes 6291460
  3.8 31.1 %copy-start.4 = (bf16[4,256,16]{1,2,0:T(8,128)(2,1)S(1)}, bf16[4,256,16]{1,2,0:T(8,128)(2,1)}, u32[]{:S(2)}) copy-start(bf16[4,256,16]{1,2,0:T(8,128)(2,1)} %param.4) | copy-start | bytes 98308
  36.4 65.0 %all-to-all-start.1 = ((bf16[64,4,256,16]{2,3,1,0:T(8,128)(2,1)}), bf16[64,4,256,16]{2,3,1,0:T(8,128)(2,1)}, u32[]{:S(2)}, u32[]{:S(2)}) async-start(bf16[64,4,256,16]{2,3,1,0:T(8,128)(2,1)} %stack.5), calls=%async_computation.1 | async-start | bytes 4194304 | tf_op jit(solution)/shard_map/all_to_all | solution.py:12
  103.2 1.3 copy-start.2
  235.2 5.8 %copy-start.1 = (f32[2,32,4,1024,16]{3,4,1,0,2:T(8,128)}, f32[2,32,4,1024,16]{3,4,1,0,2:T(8,128)S(1)}, u32[]{:S(2)}) copy-start(f32[2,32,4,1024,16]{3,4,1,0,2:T(8,128)S(1)} %convolution_bitcast_fusion) | copy-start | bytes 50331652
  395.1 25.6 %all-to-all-start.5 = ((bf16[64,2,4096]{2,1,0:T(2,128)(2,1)}), bf16[64,2,4096]{2,1,0:T(2,128)(2,1)S(1)}, u32[]{:S(2)}, u32[]{:S(2)}) async-start(bf16[64,2,4096]{2,1,0:T(2,128)(2,1)} %reshape.225), calls=%async_computation.5 | async-start | bytes 2097152 | tf_op jit(solution)/shard_map/all_to_all | solution.py:81
  424.1 3.4 copy-start.3
